TPU v7x, 128 devices: a whole 4x4x4 slice. The times are simulated.
128 devices in a mesh: rep: 32 (over y, z, x_lo), grp: 4 (over x_hi, core).
Axes of the slice: x: 4 (x_hi: 2, x_lo: 2; x = x_hi * 2 + x_lo), y: 4, z: 4, core: 2. Of those that a mesh axis runs over, the one named last changes fastest.
Arguments:
- tokens: bfloat16 [64, 1024, 768], P('rep', 'grp'), may hold values from -6 to 6
- segment: int32 [64, 1024], P('rep'), may hold values from 0 to 1, as said below
- piece_start: int32 [64, 1024], P('rep'), may hold values from 0 to 1023, as said below
- w_query: bfloat16 [768, 768], P('grp'), may hold values from -0.21875 to 0.21875
- w_key: bfloat16 [768, 768], P('grp'), may hold values from -0.21875 to 0.21875
- w_value: bfloat16 [768, 768], P('grp'), may hold values from -0.21875 to 0.21875
- w_out: bfloat16 [768, 768], P('grp'), may hold values from -3.5 to 3.5
- w_gate: bfloat16 [768, 3072], P('grp'), may hold values from -0.21875 to 0.21875
- w_up: bfloat16 [768, 3072], P('grp'), may hold values from -0.21875 to 0.21875
- w_down: bfloat16 [3072, 768], P('grp'), may hold values from -0.109375 to 0.109375
- cotangent: bfloat16 [64, 1024, 768], P('rep', 'grp'), may hold values from -6 to 6
Outputs:
- output: bfloat16 [64, 1024, 768], P('rep', 'grp')
- grad_tokens: bfloat16 [64, 1024, 768], P('rep', 'grp')
- grad_query: float32 [768, 768], P('grp')
- grad_key: float32 [768, 768], P('grp')
- grad_value: float32 [768, 768], P('grp')
- grad_out: float32 [768, 768], P('grp')
- grad_gate: float32 [768, 3072], P('grp')
- grad_up: float32 [768, 3072], P('grp')
- grad_down: float32 [3072, 768], P('grp')
Inputs may be any that keep to these rules, and one draw needn't show every extreme that they name: `segment`: along a sequence the numbers start at 0, never fall, rise by one at a time, and rise only at the first position of a picture piece. `piece_start`: each sequence holds 2 picture pieces of 256 positions, the k-th lying within positions k * (512) to (k + 1) * 512 - 1; a piece's positions hold its first position, all other positions their own.
All inputs are finite; a program needn't handle non-finite values.
Results may differ from a plain program's by a relative error of at most 0.029.
Values may be sent and summed in bfloat16 or wider, within the bound.
No kernel may reach another device: no remote copies, remote signals or barrier semaphores. Data moves between devices by JAX's collectives and lax.ppermute only.
A program may use at most 256 MiB of HBM per device.

v0:
```python
import jax
import jax.numpy as jnp
from jax import lax
from jax.sharding import PartitionSpec as P

HEADS = 12
HDIM = 64


def layer_norm(hidden):
    centred = hidden - jnp.mean(hidden, axis=-1, keepdims=True)
    spread = jnp.mean(centred * centred, axis=-1, keepdims=True)
    return centred * lax.rsqrt(spread + 1e-05)


def rotate(heads, cosine, sine):
    half = heads.shape[-1] // 2
    first = heads[..., :half]
    second = heads[..., half:]
    return jnp.concatenate(
        [first * cosine - second * sine, second * cosine + first * sine], axis=-1
    )


def gated(gate, upper):
    return gate / (1.0 + jnp.exp(-gate)) * upper


def matmul(left, right):
    return jnp.dot(left, right, preferred_element_type=jnp.float32)


def contract_rows(left, right):
    return lax.dot_general(
        left, right, (((0,), (0,)), ((), ())), preferred_element_type=jnp.float32
    )


def contract_cols(left, right):
    return lax.dot_general(
        left, right, (((1,), (1,)), ((), ())), preferred_element_type=jnp.float32
    )


def body(
    tokens, segment, piece_start, w_query, w_key, w_value, w_out, w_gate, w_up, w_down, cotangent
):
    local_length = tokens.shape[1]
    groups = lax.axis_size("grp")
    full_length = local_length * groups
    width = tokens.shape[2]
    head_count = HEADS
    head_size = HDIM
    scale = head_size ** (-0.5)
    first_row = lax.axis_index("grp") * local_length
    rows = first_row + jnp.arange(local_length, dtype=jnp.int32)
    columns = jnp.arange(full_length, dtype=jnp.int32)
    inverse = 10000.0 ** (-jnp.arange(0, head_size, 2).astype(jnp.float32) / head_size)
    angles = rows.astype(jnp.float32)[:, None] * inverse[None, :]
    cosine = jnp.cos(angles)[:, None, :]
    sine = jnp.sin(angles)[:, None, :]
    shards = (w_query, w_key, w_value, w_out, w_gate, w_up, w_down)
    totals = [jnp.zeros((shard.shape[0] * groups, shard.shape[1]), jnp.float32) for shard in shards]
    outputs = []
    input_grads = []
    for index in range(tokens.shape[0]):
        full = (
            lax.all_gather(w_query, "grp", axis=0, tiled=True),
            lax.all_gather(w_key, "grp", axis=0, tiled=True),
            lax.all_gather(w_value, "grp", axis=0, tiled=True),
            lax.all_gather(w_out, "grp", axis=0, tiled=True),
            lax.all_gather(w_gate, "grp", axis=0, tiled=True),
            lax.all_gather(w_up, "grp", axis=0, tiled=True),
            lax.all_gather(w_down, "grp", axis=0, tiled=True),
        )
        query_weight, key_weight, value_weight, out_weight, gate_weight, up_weight, down_weight = (
            full
        )
        hidden = tokens[index].astype(jnp.float32)
        normed, norm_one_back = jax.vjp(layer_norm, hidden)
        normed_low = normed.astype(jnp.bfloat16)
        query_heads = rotate(
            matmul(normed_low, query_weight).reshape(local_length, head_count, head_size),
            cosine,
            sine,
        ).astype(jnp.bfloat16)
        keys = (
            rotate(
                matmul(normed_low, key_weight).reshape(local_length, head_count, head_size),
                cosine,
                sine,
            )
            .reshape(local_length, width)
            .astype(jnp.bfloat16)
        )
        values = matmul(normed_low, value_weight).astype(jnp.bfloat16)
        all_keys, all_values = (
            lax.all_gather(keys, "grp", axis=0, tiled=True),
            lax.all_gather(values, "grp", axis=0, tiled=True),
        )
        key_heads = all_keys.reshape(full_length, head_count, head_size)
        value_heads = all_values.reshape(full_length, head_count, head_size)
        seg_row = segment[index]
        start_row = piece_start[index]
        seg_local = lax.dynamic_slice_in_dim(seg_row, first_row, local_length)
        start_local = lax.dynamic_slice_in_dim(start_row, first_row, local_length)
        causal = columns[None, :] <= rows[:, None]
        same_piece = start_local[:, None] == start_row[None, :]
        allowed = (seg_local[:, None] == seg_row[None, :]) & (causal | same_piece)

        def scores_of(heads_in):
            raw = jnp.einsum(
                "qhd,khd->hqk", heads_in, key_heads, preferred_element_type=jnp.float32
            )
            return jnp.where(allowed[None], raw * scale, -1e30)

        scores = scores_of(query_heads)
        highest = jnp.max(scores, axis=-1, keepdims=True)
        expd = jnp.exp(scores - highest)
        total = jnp.sum(expd, axis=-1, keepdims=True)
        log_total = highest + jnp.log(total)
        probs_low = (expd / total).astype(jnp.bfloat16)
        mixed = jnp.einsum(
            "hqk,khd->qhd", probs_low, value_heads, preferred_element_type=jnp.float32
        )
        mixed_low = mixed.reshape(local_length, width).astype(jnp.bfloat16)
        after = hidden + matmul(mixed_low, out_weight)
        normed_two, norm_two_back = jax.vjp(layer_norm, after)
        normed_two_low = normed_two.astype(jnp.bfloat16)
        gate = matmul(normed_two_low, gate_weight)
        upper = matmul(normed_two_low, up_weight)
        active, gate_back = jax.vjp(gated, gate, upper)
        active_low = active.astype(jnp.bfloat16)
        result = after + matmul(active_low, down_weight)
        outputs.append(result.astype(jnp.bfloat16))
        full = (
            lax.all_gather(w_query, "grp", axis=0, tiled=True),
            lax.all_gather(w_key, "grp", axis=0, tiled=True),
            lax.all_gather(w_value, "grp", axis=0, tiled=True),
            lax.all_gather(w_out, "grp", axis=0, tiled=True),
            lax.all_gather(w_gate, "grp", axis=0, tiled=True),
            lax.all_gather(w_up, "grp", axis=0, tiled=True),
            lax.all_gather(w_down, "grp", axis=0, tiled=True),
        )
        query_weight, key_weight, value_weight, out_weight, gate_weight, up_weight, down_weight = (
            full
        )
        grad_result = cotangent[index]
        totals[6] = totals[6] + contract_rows(active_low, grad_result)
        grad_active = contract_cols(grad_result, down_weight)
        grad_gate, grad_upper = gate_back(grad_active)
        gate_low = grad_gate.astype(jnp.bfloat16)
        upper_low = grad_upper.astype(jnp.bfloat16)
        totals[4] = totals[4] + contract_rows(normed_two_low, gate_low)
        totals[5] = totals[5] + contract_rows(normed_two_low, upper_low)
        grad_normed_two = contract_cols(gate_low, gate_weight) + contract_cols(upper_low, up_weight)
        grad_after = grad_result.astype(jnp.float32) + norm_two_back(grad_normed_two)[0]
        after_low = grad_after.astype(jnp.bfloat16)
        totals[3] = totals[3] + contract_rows(mixed_low, after_low)
        grad_mixed = (
            contract_cols(after_low, out_weight)
            .astype(jnp.bfloat16)
            .reshape(local_length, head_count, head_size)
        )
        probs = jnp.exp(scores_of(query_heads) - log_total)
        grad_probs = jnp.einsum(
            "qhd,khd->hqk", grad_mixed, value_heads, preferred_element_type=jnp.float32
        )
        inner = jnp.sum(probs * grad_probs, axis=-1, keepdims=True)
        grad_raw = (probs * (grad_probs - inner) * scale).astype(jnp.bfloat16)
        grad_query = jnp.einsum(
            "hqk,khd->qhd", grad_raw, key_heads, preferred_element_type=jnp.float32
        )
        again_low = probs.astype(jnp.bfloat16)
        grad_keys = jnp.einsum(
            "hqk,qhd->khd", grad_raw, query_heads, preferred_element_type=jnp.float32
        ).reshape(full_length, width)
        grad_values = jnp.einsum(
            "hqk,qhd->khd", again_low, grad_mixed, preferred_element_type=jnp.float32
        ).reshape(full_length, width)
        own_keys, own_values = (
            lax.psum_scatter(
                grad_keys.astype(jnp.bfloat16), "grp", scatter_dimension=0, tiled=True
            ).astype(jnp.float32),
            lax.psum_scatter(
                grad_values.astype(jnp.bfloat16), "grp", scatter_dimension=0, tiled=True
            ).astype(jnp.float32),
        )
        query_low = (
            rotate(grad_query, cosine, -sine).reshape(local_length, width).astype(jnp.bfloat16)
        )
        keys_low = (
            rotate(own_keys.reshape(local_length, head_count, head_size), cosine, -sine)
            .reshape(local_length, width)
            .astype(jnp.bfloat16)
        )
        values_low = own_values.astype(jnp.bfloat16)
        totals[0] = totals[0] + contract_rows(normed_low, query_low)
        totals[1] = totals[1] + contract_rows(normed_low, keys_low)
        totals[2] = totals[2] + contract_rows(normed_low, values_low)
        grad_normed = (
            contract_cols(query_low, query_weight)
            + contract_cols(keys_low, key_weight)
            + contract_cols(values_low, value_weight)
        )
        grad_hidden = grad_after + norm_one_back(grad_normed)[0]
        input_grads.append(grad_hidden.astype(jnp.bfloat16))
    owned = (
        lax.psum_scatter(
            totals[0].astype(jnp.bfloat16), "grp", scatter_dimension=0, tiled=True
        ).astype(jnp.float32),
        lax.psum_scatter(
            totals[1].astype(jnp.bfloat16), "grp", scatter_dimension=0, tiled=True
        ).astype(jnp.float32),
        lax.psum_scatter(
            totals[2].astype(jnp.bfloat16), "grp", scatter_dimension=0, tiled=True
        ).astype(jnp.float32),
        lax.psum_scatter(
            totals[3].astype(jnp.bfloat16), "grp", scatter_dimension=0, tiled=True
        ).astype(jnp.float32),
        lax.psum_scatter(
            totals[4].astype(jnp.bfloat16), "grp", scatter_dimension=0, tiled=True
        ).astype(jnp.float32),
        lax.psum_scatter(
            totals[5].astype(jnp.bfloat16), "grp", scatter_dimension=0, tiled=True
        ).astype(jnp.float32),
        lax.psum_scatter(
            totals[6].astype(jnp.bfloat16), "grp", scatter_dimension=0, tiled=True
        ).astype(jnp.float32),
    )
    summed = (
        lax.psum(owned[0].astype(jnp.bfloat16), "rep").astype(jnp.float32),
        lax.psum(owned[1].astype(jnp.bfloat16), "rep").astype(jnp.float32),
        lax.psum(owned[2].astype(jnp.bfloat16), "rep").astype(jnp.float32),
        lax.psum(owned[3].astype(jnp.bfloat16), "rep").astype(jnp.float32),
        lax.psum(owned[4].astype(jnp.bfloat16), "rep").astype(jnp.float32),
        lax.psum(owned[5].astype(jnp.bfloat16), "rep").astype(jnp.float32),
        lax.psum(owned[6].astype(jnp.bfloat16), "rep").astype(jnp.float32),
    )
    return (
        jnp.stack(outputs),
        jnp.stack(input_grads),
        summed[0],
        summed[1],
        summed[2],
        summed[3],
        summed[4],
        summed[5],
        summed[6],
    )


def solution(mesh):
    placed = (
        P("rep", "grp", None),
        P("rep", None),
        P("rep", None),
        P("grp", None),
        P("grp", None),
        P("grp", None),
        P("grp", None),
        P("grp", None),
        P("grp", None),
        P("grp", None),
        P("rep", "grp", None),
    )
    return jax.shard_map(
        body,
        mesh=mesh,
        in_specs=placed,
        out_specs=(
            P("rep", "grp", None),
            P("rep", "grp", None),
            P("grp", None),
            P("grp", None),
            P("grp", None),
            P("grp", None),
            P("grp", None),
            P("grp", None),
            P("grp", None),
        ),
        check_vma=False,
    )
```

profile of v0, /device:TPU:0, one launch (start us, length us, event | category | flops | bytes accessed | tf_op | source)
XLA Modules:
  0.0 1195.9 jit_solution(17734370692806180140)
XLA Ops:
  13.2 20.5 %all-gather.18.cloned.1.call-done = bf16[768,768]{1,0:T(8,128)(2,1)} async-done(((bf16[192,768]{1,0:T(8,128)(2,1)}), bf16[768,768]{1,0:T(8,128)(2,1)}) %all-gather.18.cloned.1.call-update) | async-done | bytes 1179664 | tf_op jit(solution)/shard_map/all_gather | solution.py:69
  35.2 21.1 %all-gather.16.cloned.1.call-done = bf16[768,768]{1,0:T(8,128)(2,1)} async-done(((bf16[192,768]{1,0:T(8,128)(2,1)}), bf16[768,768]{1,0:T(8,128)(2,1)}) %all-gather.16.cloned.1.call-update) | async-done | bytes 1179664 | tf_op jit(solution)/shard_map/all_gather | solution.py:68
  62.5 16.5 %all-gather.12.cloned.1.call-done = bf16[768,768]{1,0:T(8,128)(2,1)} async-done(((bf16[192,768]{1,0:T(8,128)(2,1)}), bf16[768,768]{1,0:T(8,128)(2,1)}) %all-gather.12.cloned.1.call-update) | async-done | bytes 1179664 | tf_op jit(solution)/shard_map/all_gather | solution.py:70
  88.7 15.6 %all-gather.32.cloned.1.call-done = bf16[1024,768]{0,1:T(8,128)(2,1)} async-done(((bf16[256,768]{0,1:T(8,128)(2,1)}), bf16[1024,768]{0,1:T(8,128)(2,1)}) %all-gather.32.cloned.1.call-update) | async-done | bytes 1572880 | tf_op jit(solution)/shard_map/all_gather | solution.py:98
  116.5 13.1 %all-gather.30.cloned.1.call-done = bf16[1024,768]{1,0:T(8,128)(2,1)} async-done(((bf16[256,768]{1,0:T(8,128)(2,1)}), bf16[1024,768]{1,0:T(8,128)(2,1)}) %all-gather.30.cloned.1.call-update) | async-done | bytes 1572880 | tf_op jit(solution)/shard_map/all_gather | solution.py:99
  138.4 16.5 %all-gather.14.cloned.1.call-done = bf16[1024,768]{1,0:T(8,128)(2,1)} async-done(((bf16[256,768]{1,0:T(8,128)(2,1)}), bf16[1024,768]{1,0:T(8,128)(2,1)}) %all-gather.14.cloned.1.call-update) | async-done | bytes 1572880 | tf_op jit(solution)/shard_map/all_gather | solution.py:99
  157.5 20.0 %all-gather.22.cloned.1.call-done = bf16[768,768]{1,0:T(8,128)(2,1)} async-done(((bf16[192,768]{1,0:T(8,128)(2,1)}), bf16[768,768]{1,0:T(8,128)(2,1)}) %all-gather.22.cloned.1.call-update) | async-done | bytes 1179664 | tf_op jit(solution)/shard_map/all_gather | solution.py:71
  180.2 22.9 %all-gather.20.cloned.1.call-done = bf16[1024,768]{0,1:T(8,128)(2,1)} async-done(((bf16[256,768]{0,1:T(8,128)(2,1)}), bf16[1024,768]{0,1:T(8,128)(2,1)}) %all-gather.20.cloned.1.call-update) | async-done | bytes 1572880 | tf_op jit(solution)/shard_map/all_gather | solution.py:98
  220.0 25.7 %all-gather.26.cloned.1.call-done = bf16[768,3072]{1,0:T(8,128)(2,1)} async-done(((bf16[192,3072]{1,0:T(8,128)(2,1)}), bf16[768,3072]{1,0:T(8,128)(2,1)}) %all-gather.26.cloned.1.call-update) | async-done | bytes 4718608 | tf_op jit(solution)/shard_map/all_gather | solution.py:73
  251.3 36.9 %all-gather.24.cloned.1.call-done = bf16[768,3072]{1,0:T(8,128)(2,1)} async-done(((bf16[192,3072]{1,0:T(8,128)(2,1)}), bf16[768,3072]{1,0:T(8,128)(2,1)}) %all-gather.24.cloned.1.call-update) | async-done | bytes 4718608 | tf_op jit(solution)/shard_map/all_gather | solution.py:72
  293.7 37.1 %all-gather.28.cloned.1.call-done = bf16[3072,768]{1,0:T(8,128)(2,1)} async-done(((bf16[768,768]{1,0:T(8,128)(2,1)}), bf16[3072,768]{1,0:T(8,128)(2,1)}) %all-gather.28.cloned.1.call-update) | async-done | bytes 4718608 | tf_op jit(solution)/shard_map/all_gather | solution.py:74
  330.8 8.3 multiply_convert_fusion.2
  363.2 9.1 fusion.66
  377.1 8.4 fusion.69
  393.6 34.9 %fusion.75 = bf16[12,64,1024]{2,1,0:T(8,128)(2,1)} fusion(f32[12,256,1024]{2,1,0:T(8,128)} %fusion.209, f32[12,256,1024]{2,1,0:T(8,128)} %copy-done.2, f32[12,256]{1,0:T(8,128)S(1)} %copy-done.71, pred[256,1024]{1,0:T(8,128)(4,1)} %copy-done.32, bf16[256,12,32]{0,2,1:T(8,128)(2,1)S(1)} %copy-done.55, bf16[256,12,32]{0,2,1:T(8,128)(2,1)S(1)} %copy-done.53), kind=kOutput, calls=%fused_computation.68 | convolution fusion | flops 438833152 | bytes 27406336 | tf_op jit(solution)/shard_map/hqk,qhd->khd/dot_general | solution.py:175
  436.9 34.6 %fusion.72 = bf16[12,64,1024]{2,1,0:T(8,128)(2,1)} fusion(f32[12,256,1024]{2,1,0:T(8,128)} %fusion.212, f32[12,256,1024]{2,1,0:T(8,128)} %copy-done.1, f32[12,256]{1,0:T(8,128)S(1)} %copy-done.73, pred[256,1024]{1,0:T(8,128)(4,1)} %copy-done.31, bf16[256,12,32]{0,2,1:T(8,128)(2,1)S(1)} %copy-done.49, bf16[256,12,32]{0,2,1:T(8,128)(2,1)S(1)} %copy-done.51), kind=kOutput, calls=%fused_computation.67 | convolution fusion | flops 438833152 | bytes 27406336 | tf_op jit(solution)/shard_map/hqk,qhd->khd/dot_general | solution.py:175
  481.7 34.6 %fusion.81 = f32[256,12,64]{0,2,1:T(8,128)} fusion(bf16[1024,12,64]{0,2,1:T(8,128)(2,1)} %bitcast.263, f32[12,256,1024]{2,1,0:T(8,128)} %fusion.209, f32[12,256,1024]{2,1,0:T(8,128)} %copy-done.2, f32[12,256]{1,0:T(8,128)S(1)} %copy-done.72, pred[256,1024]{1,0:T(8,128)(4,1)} %copy-done.32), kind=kOutput, calls=%fused_computation.70 | convolution fusion | flops 437260288 | bytes 27799552 | tf_op jit(solution)/shard_map/hqk,khd->qhd/dot_general | solution.py:171
  516.2 34.3 %fusion.78 = f32[256,12,64]{0,2,1:T(8,128)} fusion(bf16[1024,12,64]{0,2,1:T(8,128)(2,1)} %bitcast.261, f32[12,256,1024]{2,1,0:T(8,128)} %fusion.212, f32[12,256,1024]{2,1,0:T(8,128)} %copy-done.1, f32[12,256]{1,0:T(8,128)S(1)} %copy-done.74, pred[256,1024]{1,0:T(8,128)(4,1)} %copy-done.31), kind=kOutput, calls=%fused_computation.69 | convolution fusion | flops 437260288 | bytes 27799552 | tf_op jit(solution)/shard_map/hqk,khd->qhd/dot_general | solution.py:171
  588.6 34.6 %reduce-scatter.22.cloned.1.call-done = bf16[192,768]{1,0:T(8,128)(2,1)} async-done(((bf16[768,768]{1,0:T(8,128)(2,1)}), bf16[192,768]{1,0:T(8,128)(2,1)}) %reduce-scatter.22.cloned.1.call-update) | async-done | bytes 294928 | tf_op jit(solution)/shard_map/reduce_scatter | solution.py:212
  623.2 35.5 %reduce-scatter.20.cloned.1.call-done = bf16[192,768]{1,0:T(8,128)(2,1)} async-done(((bf16[768,768]{1,0:T(8,128)(2,1)}), bf16[192,768]{1,0:T(8,128)(2,1)}) %reduce-scatter.20.cloned.1.call-update) | async-done | bytes 294928 | tf_op jit(solution)/shard_map/reduce_scatter | solution.py:209
  658.7 56.7 %reduce-scatter.32.cloned.1.call-done = bf16[768,768]{1,0:T(8,128)(2,1)} async-done(((bf16[3072,768]{1,0:T(8,128)(2,1)}), bf16[768,768]{1,0:T(8,128)(2,1)}) %reduce-scatter.32.cloned.1.call-update) | async-done | bytes 1179664 | tf_op jit(solution)/shard_map/reduce_scatter | solution.py:227
  715.4 57.1 %reduce-scatter.30.cloned.1.call-done = bf16[192,3072]{1,0:T(8,128)(2,1)} async-done(((bf16[768,3072]{1,0:T(8,128)(2,1)}), bf16[192,3072]{1,0:T(8,128)(2,1)}) %reduce-scatter.30.cloned.1.call-update) | async-done | bytes 1179664 | tf_op jit(solution)/shard_map/reduce_scatter | solution.py:224
  772.5 56.9 %reduce-scatter.28.cloned.1.call-done = bf16[192,3072]{1,0:T(8,128)(2,1)} async-done(((bf16[768,3072]{1,0:T(8,128)(2,1)}), bf16[192,3072]{1,0:T(8,128)(2,1)}) %reduce-scatter.28.cloned.1.call-update) | async-done | bytes 1179664 | tf_op jit(solution)/shard_map/reduce_scatter | solution.py:221
  844.6 330.8 %all-reduce.3.cloned.1.call-done = (bf16[192,768]{1,0:T(8,128)(2,1)}, bf16[192,768]{1,0:T(8,128)(2,1)}, bf16[192,768]{1,0:T(8,128)(2,1)}, bf16[192,768]{1,0:T(8,...) async-done(((bf16[192,768]{1,0:T(8,128)(2,1)}, bf16[192,768]{1,0:T(8,128)(2,1)}, bf16[192,768]{1,0:T(8,128)(2,1)}, ...) | async-done | bytes 4718608 | tf_op jit(solution)/shard_map/psum | solution.py:232
  (360 shorter events, 198.4 us)
Async XLA Ops:
  7.2 26.5 %all-gather.18.cloned.1.call-start = ((), (), s32[]{:S(2)}) async-start(), calls=%async_computation.14 | async-start | bytes 1474560 | tf_op jit(solution)/shard_map/all_gather | solution.py:69
  7.9 48.4 %all-gather.16.cloned.1.call-start = ((), (), s32[]{:S(2)}) async-start(), calls=%async_computation.13 | async-start | bytes 1474560 | tf_op jit(solution)/shard_map/all_gather | solution.py:68
  8.7 70.3 %all-gather.12.cloned.1.call-start = ((), (), s32[]{:S(2)}) async-start(), calls=%async_computation.11 | async-start | bytes 1474560 | tf_op jit(solution)/shard_map/all_gather | solution.py:70
  9.4 95.0 %all-gather.32.cloned.1.call-start = ((), (), s32[]{:S(2)}) async-start(), calls=%async_computation.21 | async-start | bytes 1966080 | tf_op jit(solution)/shard_map/all_gather | solution.py:98
  62.4 67.2 %all-gather.30.cloned.1.call-start = ((), (), s32[]{:S(2)}) async-start(), calls=%async_computation.20 | async-start | bytes 1966080 | tf_op jit(solution)/shard_map/all_gather | solution.py:99
  81.5 73.4 %all-gather.14.cloned.1.call-start = ((), (), s32[]{:S(2)}) async-start(), calls=%async_computation.12 | async-start | bytes 1966080 | tf_op jit(solution)/shard_map/all_gather | solution.py:99
  84.2 93.4 %all-gather.22.cloned.1.call-start = ((), (), s32[]{:S(2)}) async-start(), calls=%async_computation.16 | async-start | bytes 1474560 | tf_op jit(solution)/shard_map/all_gather | solution.py:71
  84.9 118.2 %all-gather.20.cloned.1.call-start = ((), (), s32[]{:S(2)}) async-start(), calls=%async_computation.15 | async-start | bytes 1966080 | tf_op jit(solution)/shard_map/all_gather | solution.py:98
  85.8 160.0 %all-gather.26.cloned.1.call-start = ((), (), s32[]{:S(2)}) async-start(), calls=%async_computation.18 | async-start | bytes 5898240 | tf_op jit(solution)/shard_map/all_gather | solution.py:73
  86.5 201.7 %all-gather.24.cloned.1.call-start = ((), (), s32[]{:S(2)}) async-start(), calls=%async_computation.17 | async-start | bytes 5898240 | tf_op jit(solution)/shard_map/all_gather | solution.py:72
  87.1 243.8 %all-gather.28.cloned.1.call-start = ((), (), s32[]{:S(2)}) async-start(), calls=%async_computation.19 | async-start | bytes 5898240 | tf_op jit(solution)/shard_map/all_gather | solution.py:74
  87.8 387.0 %reduce-scatter.14.cloned.1.call-start = ((), (), s32[]{:S(2)}) async-start(), calls=%async_computation.23 | async-start | bytes 1966080 | tf_op jit(solution)/shard_map/reduce_scatter | solution.py:185
  88.7 121.8 %copy-start.32 = (pred[256,1024]{1,0:T(8,128)(4,1)}, pred[256,1024]{1,0:T(8,128)(4,1)S(1)}, u32[]{:S(2)}) copy-start(pred[256,1024]{1,0:T(8,128)(4,1)S(1)} %get-tuple-element.73) | copy-start | bytes 786436
  372.3 105.6 %reduce-scatter.18.cloned.1.call-start = ((), (), s32[]{:S(2)}) async-start(), calls=%async_computation.25 | async-start | bytes 1966080 | tf_op jit(solution)/shard_map/reduce_scatter | solution.py:185
  385.5 165.1 %reduce-scatter.12.cloned.1.call-start = ((), (), s32[]{:S(2)}) async-start(), calls=%async_computation.22 | async-start | bytes 1966080 | tf_op jit(solution)/shard_map/reduce_scatter | solution.py:182
  428.6 123.1 %reduce-scatter.16.cloned.1.call-start = ((), (), s32[]{:S(2)}) async-start(), calls=%async_computation.24 | async-start | bytes 1966080 | tf_op jit(solution)/shard_map/reduce_scatter | solution.py:182
  471.5 112.7 %reduce-scatter.26.cloned.1.call-start = ((), (), s32[]{:S(2)}) async-start(), calls=%async_computation.29 | async-start | bytes 1474560 | tf_op jit(solution)/shard_map/reduce_scatter | solution.py:218
  474.7 113.9 %reduce-scatter.24.cloned.1.call-start = ((), (), s32[]{:S(2)}) async-start(), calls=%async_computation.28 | async-start | bytes 1474560 | tf_op jit(solution)/shard_map/reduce_scatter | solution.py:215
  481.4 141.8 %reduce-scatter.22.cloned.1.call-start = ((), (), s32[]{:S(2)}) async-start(), calls=%async_computation.27 | async-start | bytes 1474560 | tf_op jit(solution)/shard_map/reduce_scatter | solution.py:212
  558.7 100.0 %reduce-scatter.20.cloned.1.call-start = ((), (), s32[]{:S(2)}) async-start(), calls=%async_computation.26 | async-start | bytes 1474560 | tf_op jit(solution)/shard_map/reduce_scatter | solution.py:209
  562.6 152.8 %reduce-scatter.32.cloned.1.call-start = ((), (), s32[]{:S(2)}) async-start(), calls=%async_computation.32 | async-start | bytes 5898240 | tf_op jit(solution)/shard_map/reduce_scatter | solution.py:227
  569.3 203.1 %reduce-scatter.30.cloned.1.call-start = ((), (), s32[]{:S(2)}) async-start(), calls=%async_computation.31 | async-start | bytes 5898240 | tf_op jit(solution)/shard_map/reduce_scatter | solution.py:224
  577.0 252.3 %reduce-scatter.28.cloned.1.call-start = ((), (), s32[]{:S(2)}) async-start(), calls=%async_computation.30 | async-start | bytes 5898240 | tf_op jit(solution)/shard_map/reduce_scatter | solution.py:221
  583.9 591.4 %all-reduce.3.cloned.1.call-start = ((), (), s32[]{:S(2)}) async-start(), calls=%async_computation.33 | async-start | bytes 9437184 | tf_op jit(solution)/shard_map/psum | solution.py:232
  (97 other events, 1110.6 us)
Sparse Core Ops, SparseCore 0:
  9.7 23.9 all-gather.17
  35.3 20.9 all-gather.15
  58.0 20.9 all-gather.11
  81.0 23.2 all-gather.31
  106.5 23.1 all-gather.29
  131.7 23.1 all-gather.13
  156.5 20.9 all-gather.21
  179.7 23.2 all-gather.19
  204.8 40.9 all-gather.25
  247.2 40.9 all-gather.23
  289.9 40.9 all-gather.27
  372.4 34.5 reduce-scatter.13
  409.8 34.6 reduce-scatter.17
  447.0 34.6 reduce-scatter.11
  484.4 34.6 reduce-scatter.15
  521.6 32.2 reduce-scatter.25
  556.5 31.9 reduce-scatter.23
  591.1 32.0 reduce-scatter.21
  626.6 32.0 reduce-scatter.19
  661.2 54.1 reduce-scatter.31
  718.2 54.1 reduce-scatter.29
  775.1 54.1 reduce-scatter.27
  832.7 342.6 all-reduce.2
where the time goes:
time: 1200 us
  waiting for transfers between devices  827 us (69%)
  matrix products  285 us (24%)
  other arithmetic  44 us (4%)
  local copies, waits for them, and re-layouts  21.7 us (2%)
  between operations  16 us (1%)
    psum x1, waiting for transfers between devices, body(): lax.psum(owned[0].astype(jnp.bfloat16), 'rep').astype(jnp.float32)  331 us
    dot_general x2, matrix products, body(): jnp.einsum('hqk,qhd->khd', grad_raw, query_heads, preferred_element_type=...  69.5 us
    dot_general x2, matrix products, body(): jnp.einsum('hqk,khd->qhd', grad_raw, key_heads, preferred_element_type=jn...  68.9 us
    reduce_scatter x1, waiting for transfers between devices, body(): lax.psum_scatter(totals[5].astype(jnp.bfloat16), 'grp', scatter_dimension...  57.1 us
    reduce_scatter x1, waiting for transfers between devices, body(): lax.psum_scatter(totals[4].astype(jnp.bfloat16), 'grp', scatter_dimension...  56.9 us
    reduce_scatter x1, waiting for transfers between devices, body(): lax.psum_scatter(totals[6].astype(jnp.bfloat16), 'grp', scatter_dimension...  56.7 us
    all_gather x2, waiting for transfers between devices, body(): lax.all_gather(keys, 'grp', axis=0, tiled=True)  38.6 us
    all_gather x1, waiting for transfers between devices, body(): lax.all_gather(w_down, 'grp', axis=0, tiled=True)  37.1 us
  transfers between devices with their start and end apart: 23, of which 18 were waited for; matrix products, arithmetic and copies ran while one was open for 24% of the time, Pallas kernels for 0%

commit v1 on v0

--- a/solution.py
+++ b/solution.py
@@ -229,7 +229,7 @@
         ).astype(jnp.float32),
     )
     summed = (
-        lax.psum(owned[0].astype(jnp.bfloat16), "rep").astype(jnp.float32),
+        jnp.sum(lax.all_gather(owned[0].astype(jnp.bfloat16), "rep"), axis=0).astype(jnp.float32),
         lax.psum(owned[1].astype(jnp.bfloat16), "rep").astype(jnp.float32),
         lax.psum(owned[2].astype(jnp.bfloat16), "rep").astype(jnp.float32),
         lax.psum(owned[3].astype(jnp.bfloat16), "rep").astype(jnp.float32),

time: 1200 us -> 1410 us (1.18)
  waiting for transfers between devices: 827 us -> 1030 us
    all_gather x0 -> x1, waiting for transfers between devices: none -> 202 us  [body(): lax.all_gather(owned[0].astype(jnp.bfloat16), 'rep')]
  transfers between devices with their start and end apart: 23 -> 24, of which waited for: 18 -> 19; matrix products, arithmetic and copies ran while one was open for 24% -> 21% of each run, Pallas kernels for 0% -> 0%
where the time goes in v1:
time: 1410 us; the launch traced here: 1400 us
  waiting for transfers between devices  1030 us (73%)
  matrix products  285 us (20%)
  other arithmetic  48.3 us (3%)
  local copies, waits for them, and re-layouts  21.9 us (2%)
  between operations  16.3 us (1%)
    psum x1, waiting for transfers between devices, body(): lax.psum(owned[1].astype(jnp.bfloat16), 'rep').astype(jnp.float32)  327 us
    all_gather x1, waiting for transfers between devices, body(): lax.all_gather(owned[0].astype(jnp.bfloat16), 'rep')  202 us
    dot_general x2, matrix products, body(): jnp.einsum('hqk,qhd->khd', grad_raw, query_heads, preferred_element_type=...  69.5 us
    dot_general x2, matrix products, body(): jnp.einsum('hqk,khd->qhd', grad_raw, key_heads, preferred_element_type=jn...  68.9 us
    reduce_scatter x1, waiting for transfers between devices, body(): lax.psum_scatter(totals[4].astype(jnp.bfloat16), 'grp', scatter_dimension...  57 us
    reduce_scatter x1, waiting for transfers between devices, body(): lax.psum_scatter(totals[6].astype(jnp.bfloat16), 'grp', scatter_dimension...  57 us
    reduce_scatter x1, waiting for transfers between devices, body(): lax.psum_scatter(totals[5].astype(jnp.bfloat16), 'grp', scatter_dimension...  56.7 us
    all_gather x2, waiting for transfers between devices, body(): lax.all_gather(keys, 'grp', axis=0, tiled=True)  38.6 us
  transfers between devices with their start and end apart: 24, of which 19 were waited for; matrix products, arithmetic and copies ran while one was open for 21% of the time, Pallas kernels for 0%

profile of v1, /device:TPU:0, one launch (start us, length us, event | category | flops | bytes accessed | tf_op | source)
XLA Modules:
  0.0 1399.2 jit_solution(6125603502060836671)
XLA Ops:
  13.2 20.5 %all-gather.20.cloned.1.call-done = bf16[768,768]{1,0:T(8,128)(2,1)} async-done(((bf16[192,768]{1,0:T(8,128)(2,1)}), bf16[768,768]{1,0:T(8,128)(2,1)}) %all-gather.20.cloned.1.call-update) | async-done | bytes 1179664 | tf_op jit(solution)/shard_map/all_gather | solution.py:69
  35.2 21.1 %all-gather.18.cloned.1.call-done = bf16[768,768]{1,0:T(8,128)(2,1)} async-done(((bf16[192,768]{1,0:T(8,128)(2,1)}), bf16[768,768]{1,0:T(8,128)(2,1)}) %all-gather.18.cloned.1.call-update) | async-done | bytes 1179664 | tf_op jit(solution)/shard_map/all_gather | solution.py:68
  62.5 16.5 %all-gather.14.cloned.1.call-done = bf16[768,768]{1,0:T(8,128)(2,1)} async-done(((bf16[192,768]{1,0:T(8,128)(2,1)}), bf16[768,768]{1,0:T(8,128)(2,1)}) %all-gather.14.cloned.1.call-update) | async-done | bytes 1179664 | tf_op jit(solution)/shard_map/all_gather | solution.py:70
  88.7 15.6 %all-gather.34.cloned.1.call-done = bf16[1024,768]{0,1:T(8,128)(2,1)} async-done(((bf16[256,768]{0,1:T(8,128)(2,1)}), bf16[1024,768]{0,1:T(8,128)(2,1)}) %all-gather.34.cloned.1.call-update) | async-done | bytes 1572880 | tf_op jit(solution)/shard_map/all_gather | solution.py:98
  116.5 13.1 all-gather.32.cloned.1.call-done
  138.4 16.5 %all-gather.16.cloned.1.call-done = bf16[1024,768]{1,0:T(8,128)(2,1)} async-done(((bf16[256,768]{1,0:T(8,128)(2,1)}), bf16[1024,768]{1,0:T(8,128)(2,1)}) %all-gather.16.cloned.1.call-update) | async-done | bytes 1572880 | tf_op jit(solution)/shard_map/all_gather | solution.py:99
  157.5 20.0 %all-gather.24.cloned.1.call-done = bf16[768,768]{1,0:T(8,128)(2,1)} async-done(((bf16[192,768]{1,0:T(8,128)(2,1)}), bf16[768,768]{1,0:T(8,128)(2,1)}) %all-gather.24.cloned.1.call-update) | async-done | bytes 1179664 | tf_op jit(solution)/shard_map/all_gather | solution.py:71
  180.2 22.9 %all-gather.22.cloned.1.call-done = bf16[1024,768]{0,1:T(8,128)(2,1)} async-done(((bf16[256,768]{0,1:T(8,128)(2,1)}), bf16[1024,768]{0,1:T(8,128)(2,1)}) %all-gather.22.cloned.1.call-update) | async-done | bytes 1572880 | tf_op jit(solution)/shard_map/all_gather | solution.py:98
  220.0 25.7 %all-gather.28.cloned.1.call-done = bf16[768,3072]{1,0:T(8,128)(2,1)} async-done(((bf16[192,3072]{1,0:T(8,128)(2,1)}), bf16[768,3072]{1,0:T(8,128)(2,1)}) %all-gather.28.cloned.1.call-update) | async-done | bytes 4718608 | tf_op jit(solution)/shard_map/all_gather | solution.py:73
  251.3 36.9 %all-gather.26.cloned.1.call-done = bf16[768,3072]{1,0:T(8,128)(2,1)} async-done(((bf16[192,3072]{1,0:T(8,128)(2,1)}), bf16[768,3072]{1,0:T(8,128)(2,1)}) %all-gather.26.cloned.1.call-update) | async-done | bytes 4718608 | tf_op jit(solution)/shard_map/all_gather | solution.py:72
  293.7 37.1 %all-gather.30.cloned.1.call-done = bf16[3072,768]{1,0:T(8,128)(2,1)} async-done(((bf16[768,768]{1,0:T(8,128)(2,1)}), bf16[3072,768]{1,0:T(8,128)(2,1)}) %all-gather.30.cloned.1.call-update) | async-done | bytes 4718608 | tf_op jit(solution)/shard_map/all_gather | solution.py:74
  363.2 9.1 fusion.66
  377.1 8.4 fusion.69
  393.6 34.9 %fusion.75 = bf16[12,64,1024]{2,1,0:T(8,128)(2,1)} fusion(f32[12,256,1024]{2,1,0:T(8,128)} %fusion.209, f32[12,256,1024]{2,1,0:T(8,128)} %copy-done.2, f32[12,256]{1,0:T(8,128)S(1)} %copy-done.71, pred[256,1024]{1,0:T(8,128)(4,1)} %copy-done.30, bf16[256,12,32]{0,2,1:T(8,128)(2,1)S(1)} %copy-done.53, bf16[256,12,32]{0,2,1:T(8,128)(2,1)S(1)} %copy-done.51), kind=kOutput, calls=%fused_computation.68 | convolution fusion | flops 438833152 | bytes 27406336 | tf_op jit(solution)/shard_map/hqk,qhd->khd/dot_general | solution.py:175
  436.9 34.6 %fusion.72 = bf16[12,64,1024]{2,1,0:T(8,128)(2,1)} fusion(f32[12,256,1024]{2,1,0:T(8,128)} %fusion.212, f32[12,256,1024]{2,1,0:T(8,128)} %copy-done.1, f32[12,256]{1,0:T(8,128)S(1)} %copy-done.73, pred[256,1024]{1,0:T(8,128)(4,1)} %copy-done.29, bf16[256,12,32]{0,2,1:T(8,128)(2,1)S(1)} %copy-done.47, bf16[256,12,32]{0,2,1:T(8,128)(2,1)S(1)} %copy-done.49), kind=kOutput, calls=%fused_computation.67 | convolution fusion | flops 438833152 | bytes 27406336 | tf_op jit(solution)/shard_map/hqk,qhd->khd/dot_general | solution.py:175
  481.7 34.5 %fusion.81 = f32[256,12,64]{0,2,1:T(8,128)} fusion(bf16[1024,12,64]{0,2,1:T(8,128)(2,1)} %bitcast.265, f32[12,256,1024]{2,1,0:T(8,128)} %fusion.209, f32[12,256,1024]{2,1,0:T(8,128)} %copy-done.2, f32[12,256]{1,0:T(8,128)S(1)} %copy-done.72, pred[256,1024]{1,0:T(8,128)(4,1)} %copy-done.30), kind=kOutput, calls=%fused_computation.70 | convolution fusion | flops 437260288 | bytes 27799552 | tf_op jit(solution)/shard_map/hqk,khd->qhd/dot_general | solution.py:171
  516.2 34.4 %fusion.78 = f32[256,12,64]{0,2,1:T(8,128)} fusion(bf16[1024,12,64]{0,2,1:T(8,128)(2,1)} %bitcast.263, f32[12,256,1024]{2,1,0:T(8,128)} %fusion.212, f32[12,256,1024]{2,1,0:T(8,128)} %copy-done.1, f32[12,256]{1,0:T(8,128)S(1)} %copy-done.74, pred[256,1024]{1,0:T(8,128)(4,1)} %copy-done.29), kind=kOutput, calls=%fused_computation.69 | convolution fusion | flops 437260288 | bytes 27799552 | tf_op jit(solution)/shard_map/hqk,khd->qhd/dot_general | solution.py:171
  588.6 34.6 %reduce-scatter.22.cloned.1.call-done = bf16[192,768]{1,0:T(8,128)(2,1)} async-done(((bf16[768,768]{1,0:T(8,128)(2,1)}), bf16[192,768]{1,0:T(8,128)(2,1)}) %reduce-scatter.22.cloned.1.call-update) | async-done | bytes 294928 | tf_op jit(solution)/shard_map/reduce_scatter | solution.py:212
  623.2 57.0 %reduce-scatter.32.cloned.1.call-done = bf16[768,768]{1,0:T(8,128)(2,1)} async-done(((bf16[3072,768]{1,0:T(8,128)(2,1)}), bf16[768,768]{1,0:T(8,128)(2,1)}) %reduce-scatter.32.cloned.1.call-update) | async-done | bytes 1179664 | tf_op jit(solution)/shard_map/reduce_scatter | solution.py:227
  680.2 56.7 %reduce-scatter.30.cloned.1.call-done = bf16[192,3072]{1,0:T(8,128)(2,1)} async-done(((bf16[768,3072]{1,0:T(8,128)(2,1)}), bf16[192,3072]{1,0:T(8,128)(2,1)}) %reduce-scatter.30.cloned.1.call-update) | async-done | bytes 1179664 | tf_op jit(solution)/shard_map/reduce_scatter | solution.py:224
  736.9 57.0 %reduce-scatter.28.cloned.1.call-done = bf16[192,3072]{1,0:T(8,128)(2,1)} async-done(((bf16[768,3072]{1,0:T(8,128)(2,1)}), bf16[192,3072]{1,0:T(8,128)(2,1)}) %reduce-scatter.28.cloned.1.call-update) | async-done | bytes 1179664 | tf_op jit(solution)/shard_map/reduce_scatter | solution.py:221
  794.2 35.0 %reduce-scatter.20.cloned.1.call-done = bf16[192,768]{1,0:T(8,128)(2,1)} async-done(((bf16[768,768]{1,0:T(8,128)(2,1)}), bf16[192,768]{1,0:T(8,128)(2,1)}) %reduce-scatter.20.cloned.1.call-update) | async-done | bytes 294928 | tf_op jit(solution)/shard_map/reduce_scatter | solution.py:209
  844.5 327.1 %all-reduce.3.cloned.1.call-done = (bf16[192,768]{1,0:T(8,128)(2,1)}, bf16[192,768]{1,0:T(8,128)(2,1)}, bf16[192,768]{1,0:T(8,128)(2,1)}, bf16[192,3072]{1,0:T(8...) async-done(((bf16[192,768]{1,0:T(8,128)(2,1)}, bf16[192,768]{1,0:T(8,128)(2,1)}, bf16[192,768]{1,0:T(8,128)(2,1)}, bf16[192,3072]{1,0:T(8,128)(2,1)}, ...) | async-done | bytes 4423696 | tf_op jit(solution)/shard_map/psum | solution.py:233
  1183.4 202.4 %all-gather.36.cloned.1.call-done = bf16[6144,768]{1,0:T(8,128)(2,1)} async-done(((bf16[192,768]{1,0:T(8,128)(2,1)}), bf16[6144,768]{1,0:T(8,128)(2,1)}) %all-gather.36.cloned.1.call-update) | async-done | bytes 9437200 | tf_op jit(solution)/shard_map/all_gather | solution.py:232
  (364 shorter events, 211.2 us)
Async XLA Ops:
  7.2 26.5 %all-gather.20.cloned.1.call-start = ((), (), s32[]{:S(2)}) async-start(), calls=%async_computation.14 | async-start | bytes 1474560 | tf_op jit(solution)/shard_map/all_gather | solution.py:69
  7.9 48.4 %all-gather.18.cloned.1.call-start = ((), (), s32[]{:S(2)}) async-start(), calls=%async_computation.13 | async-start | bytes 1474560 | tf_op jit(solution)/shard_map/all_gather | solution.py:68
  8.7 70.3 %all-gather.14.cloned.1.call-start = ((), (), s32[]{:S(2)}) async-start(), calls=%async_computation.11 | async-start | bytes 1474560 | tf_op jit(solution)/shard_map/all_gather | solution.py:70
  9.4 95.0 %all-gather.34.cloned.1.call-start = ((), (), s32[]{:S(2)}) async-start(), calls=%async_computation.21 | async-start | bytes 1966080 | tf_op jit(solution)/shard_map/all_gather | solution.py:98
  62.4 67.2 %all-gather.32.cloned.1.call-start = ((), (), s32[]{:S(2)}) async-start(), calls=%async_computation.20 | async-start | bytes 1966080 | tf_op jit(solution)/shard_map/all_gather | solution.py:99
  81.5 73.4 %all-gather.16.cloned.1.call-start = ((), (), s32[]{:S(2)}) async-start(), calls=%async_computation.12 | async-start | bytes 1966080 | tf_op jit(solution)/shard_map/all_gather | solution.py:99
  84.2 93.4 %all-gather.24.cloned.1.call-start = ((), (), s32[]{:S(2)}) async-start(), calls=%async_computation.16 | async-start | bytes 1474560 | tf_op jit(solution)/shard_map/all_gather | solution.py:71
  84.9 118.2 %all-gather.22.cloned.1.call-start = ((), (), s32[]{:S(2)}) async-start(), calls=%async_computation.15 | async-start | bytes 1966080 | tf_op jit(solution)/shard_map/all_gather | solution.py:98
  85.8 160.0 %all-gather.28.cloned.1.call-start = ((), (), s32[]{:S(2)}) async-start(), calls=%async_computation.18 | async-start | bytes 5898240 | tf_op jit(solution)/shard_map/all_gather | solution.py:73
  86.5 201.7 %all-gather.26.cloned.1.call-start = ((), (), s32[]{:S(2)}) async-start(), calls=%async_computation.17 | async-start | bytes 5898240 | tf_op jit(solution)/shard_map/all_gather | solution.py:72
  87.1 243.8 %all-gather.30.cloned.1.call-start = ((), (), s32[]{:S(2)}) async-start(), calls=%async_computation.19 | async-start | bytes 5898240 | tf_op jit(solution)/shard_map/all_gather | solution.py:74
  87.8 387.0 %reduce-scatter.14.cloned.1.call-start = ((), (), s32[]{:S(2)}) async-start(), calls=%async_computation.23 | async-start | bytes 1966080 | tf_op jit(solution)/shard_map/reduce_scatter | solution.py:185
  372.3 105.6 %reduce-scatter.18.cloned.1.call-start = ((), (), s32[]{:S(2)}) async-start(), calls=%async_computation.25 | async-start | bytes 1966080 | tf_op jit(solution)/shard_map/reduce_scatter | solution.py:185
  385.5 165.0 %reduce-scatter.12.cloned.1.call-start = ((), (), s32[]{:S(2)}) async-start(), calls=%async_computation.22 | async-start | bytes 1966080 | tf_op jit(solution)/shard_map/reduce_scatter | solution.py:182
  428.6 123.1 %reduce-scatter.16.cloned.1.call-start = ((), (), s32[]{:S(2)}) async-start(), calls=%async_computation.24 | async-start | bytes 1966080 | tf_op jit(solution)/shard_map/reduce_scatter | solution.py:182
  471.5 112.5 %reduce-scatter.26.cloned.1.call-start = ((), (), s32[]{:S(2)}) async-start(), calls=%async_computation.29 | async-start | bytes 1474560 | tf_op jit(solution)/shard_map/reduce_scatter | solution.py:218
  474.7 113.8 %reduce-scatter.24.cloned.1.call-start = ((), (), s32[]{:S(2)}) async-start(), calls=%async_computation.28 | async-start | bytes 1474560 | tf_op jit(solution)/shard_map/reduce_scatter | solution.py:215
  481.4 141.7 %reduce-scatter.22.cloned.1.call-start = ((), (), s32[]{:S(2)}) async-start(), calls=%async_computation.27 | async-start | bytes 1474560 | tf_op jit(solution)/shard_map/reduce_scatter | solution.py:212
  558.0 122.2 %reduce-scatter.32.cloned.1.call-start = ((), (), s32[]{:S(2)}) async-start(), calls=%async_computation.32 | async-start | bytes 5898240 | tf_op jit(solution)/shard_map/reduce_scatter | solution.py:227
  564.9 172.0 %reduce-scatter.30.cloned.1.call-start = ((), (), s32[]{:S(2)}) async-start(), calls=%async_computation.31 | async-start | bytes 5898240 | tf_op jit(solution)/shard_map/reduce_scatter | solution.py:224
  572.6 221.3 %reduce-scatter.28.cloned.1.call-start = ((), (), s32[]{:S(2)}) async-start(), calls=%async_computation.30 | async-start | bytes 5898240 | tf_op jit(solution)/shard_map/reduce_scatter | solution.py:221
  579.4 249.9 %reduce-scatter.20.cloned.1.call-start = ((), (), s32[]{:S(2)}) async-start(), calls=%async_computation.26 | async-start | bytes 1474560 | tf_op jit(solution)/shard_map/reduce_scatter | solution.py:209
  584.0 587.7 %all-reduce.3.cloned.1.call-start = ((), (), s32[]{:S(2)}) async-start(), calls=%async_computation.34 | async-start | bytes 8847360 | tf_op jit(solution)/shard_map/psum | solution.py:233
  793.9 591.9 %all-gather.36.cloned.1.call-start = ((), (), s32[]{:S(2)}) async-start(), calls=%async_computation.33 | async-start | bytes 9732096 | tf_op jit(solution)/shard_map/all_gather | solution.py:232
  (98 other events, 1224.8 us)
Sparse Core Ops, SparseCore 0:
  9.7 23.9 all-gather.19
  35.3 20.9 all-gather.17
  58.0 20.9 all-gather.13
  81.0 23.2 all-gather.33
  106.5 23.1 all-gather.31
  131.7 23.1 all-gather.15
  156.5 20.9 all-gather.23
  179.7 23.2 all-gather.21
  204.8 40.9 all-gather.27
  247.2 40.9 all-gather.25
  289.9 40.9 all-gather.29
  372.4 34.5 reduce-scatter.13
  409.8 34.6 reduce-scatter.17
  447.0 34.6 reduce-scatter.11
  484.4 34.5 reduce-scatter.15
  521.5 32.2 reduce-scatter.25
  556.5 32.0 reduce-scatter.23
  591.1 32.0 reduce-scatter.21
  626.0 54.1 reduce-scatter.31
  682.7 54.1 reduce-scatter.29
  739.7 54.1 reduce-scatter.27
  797.2 32.0 reduce-scatter.19
  832.5 339.0 all-reduce.2
  1173.1 212.6 all-gather.35
